TPU v7x, 32 devices: a whole 2x2x4 slice. The times are simulated.
32 devices in a mesh: chan: 8 (over z, y), facet: 4 (over x, core).
Axes of the slice: x: 2, y: 2, z: 4, core: 2. Of those that a mesh axis runs over, the one named last changes fastest.
Arguments:
- solution: float32 [8, 2048, 2048], P('chan', 'facet'), may hold values from -6 to 6
- residual: float32 [8, 2048, 2048], P('chan', 'facet'), may hold values from -120 to 120
- direction: float32 [8, 2048, 2048], P('chan', 'facet'), may hold values from -120 to 120
- spectra: float32 [8, 4096, 4096], P('chan', None, 'facet'), may hold values from 0.05 to 1
- basis: float32 [8, 8], replicated, may hold values from -2 to 2
- slot_channel: int32 [8], replicated, may hold values from 0 to 7, each once
Outputs:
- new_solution: float32 [8, 2048, 2048], P('chan', 'facet')
- new_residual: float32 [8, 2048, 2048], P('chan', 'facet')
- new_direction: float32 [8, 2048, 2048], P('chan', 'facet')
Inputs may be any that keep to these rules, and one draw needn't show every extreme that they name: `slot_channel`: every channel appears in exactly one slot.
All inputs are finite; a program needn't handle non-finite values.
Results may differ from a plain program's by a relative error of at most 0.000064.
Values sent between devices are 32-bit elements; how exact they have to be, the bound alone decides.
A program may use at most 256 MiB of HBM per device.

v0:
```python
import math
import jax
import jax.numpy as jnp
from jax import lax
from jax.sharding import PartitionSpec as P

ROOT = 64
HIGHEST = lax.Precision.HIGHEST
PRIOR_FLOOR = 0.25


def twiddle_table(left_size, right_size, length, direction_sign):
    product = (
        jnp.arange(left_size, dtype=jnp.int32)[:, None]
        * jnp.arange(right_size, dtype=jnp.int32)[None, :]
        % length
    )
    angles = product.astype(jnp.float32) * (2.0 * math.pi / length)
    return (jnp.cos(angles), direction_sign * jnp.sin(angles))


def complex_table(left_size, right_size, length, direction_sign):
    table_real, table_imag = twiddle_table(left_size, right_size, length, direction_sign)
    return jnp.stack([jnp.stack([table_real, table_imag]), jnp.stack([-table_imag, table_real])])


def real_table(left_size, right_size, length, direction_sign):
    table_real, table_imag = twiddle_table(left_size, right_size, length, direction_sign)
    return jnp.stack([table_real, table_imag])


def twisted(stacked, factor, direction_sign):
    table_real, table_imag = twiddle_table(factor, factor, factor * factor, direction_sign)
    table_real = table_real[:, :, None]
    table_imag = table_imag[:, :, None]
    real_in, imag_in = (stacked[0], stacked[1])
    return jnp.stack(
        [real_in * table_real - imag_in * table_imag, real_in * table_imag + imag_in * table_real]
    )


def forward_columns(planes, factor):
    halved = factor // 2
    groups, height = (planes.shape[0], planes.shape[1])
    blocks = planes.reshape(groups, height, halved, factor)
    section_one = jnp.einsum(
        "grjn,qjk->qgknr", blocks, real_table(halved, factor, factor, -1.0), precision=HIGHEST
    )
    section_one = twisted(section_one, factor, -1.0)
    second = jnp.einsum(
        "pgknr,pqnj->qgjkr",
        section_one,
        complex_table(factor, factor, factor, -1.0),
        precision=HIGHEST,
    )
    return second.reshape(2, groups, factor * factor, height)


def forward_rows(stacked, factor):
    halved = factor // 2
    groups, width = (stacked.shape[1], stacked.shape[2])
    blocks = stacked.reshape(2, groups, width, halved, factor)
    section_one = jnp.einsum(
        "pgcjn,pqjk->qgknc", blocks, complex_table(halved, factor, factor, -1.0), precision=HIGHEST
    )
    section_one = twisted(section_one, factor, -1.0)
    second = jnp.einsum(
        "pgknc,pqnj->qgjkc",
        section_one,
        complex_table(factor, factor, factor, -1.0),
        precision=HIGHEST,
    )
    return second.reshape(2, groups, factor * factor, width)


def inverse_rows(stacked, factor):
    halved = factor // 2
    groups, width = (stacked.shape[1], stacked.shape[3])
    blocks = stacked.reshape(2, groups, factor, factor, width)
    section_one = jnp.einsum(
        "pgjkc,pqjn->qgnkc", blocks, complex_table(factor, factor, factor, 1.0), precision=HIGHEST
    )
    section_one = twisted(section_one, factor, 1.0)
    second = jnp.einsum(
        "pgnkc,pqkj->qgjnc",
        section_one,
        complex_table(factor, halved, factor, 1.0),
        precision=HIGHEST,
    )
    return second.reshape(2, groups, halved * factor, width)


def inverse_columns(stacked, factor):
    halved = factor // 2
    groups, height = (stacked.shape[1], stacked.shape[2])
    blocks = stacked.reshape(2, groups, height, factor, factor)
    section_one = jnp.einsum(
        "pgrjk,pqjn->qgnkr", blocks, complex_table(factor, factor, factor, 1.0), precision=HIGHEST
    )
    section_one = twisted(section_one, factor, 1.0)
    table_real, table_imag = twiddle_table(factor, halved, factor, 1.0)
    last_table = jnp.stack([table_real, -table_imag])
    real_out = jnp.einsum("pgnkr,pkj->grjn", section_one, last_table, precision=HIGHEST)
    scaling = 1.0 / float(factor**4)
    return real_out.reshape(groups, height, halved * factor) * scaling


def body(solution, residual, direction, spectra, basis, slot_channel):
    channel_count = basis.shape[0]
    columns = forward_columns(direction, ROOT)
    swapped = lax.all_to_all(columns, "facet", split_axis=2, concat_axis=3, tiled=True)
    row_spectra = forward_rows(swapped, ROOT)
    weighted = row_spectra * spectra[None]
    inverted = inverse_rows(weighted, ROOT)
    returned = lax.all_to_all(inverted, "facet", split_axis=2, concat_axis=3, tiled=True)
    blurred = inverse_columns(returned, ROOT)
    regrouped = lax.all_to_all(direction, "chan", split_axis=2, concat_axis=0, tiled=True)
    one_hot = (slot_channel[:, None] == jnp.arange(channel_count, dtype=jnp.int32)[None, :]).astype(
        jnp.float32
    )
    loadings = jnp.dot(one_hot, basis, precision=HIGHEST)
    coeffs = jnp.einsum("cq,cij->qij", loadings, regrouped, precision=HIGHEST)
    local_prior = PRIOR_FLOOR * regrouped + jnp.einsum(
        "cq,qij->cij", loadings, coeffs, precision=HIGHEST
    )
    prior_term = lax.all_to_all(local_prior, "chan", split_axis=0, concat_axis=2, tiled=True)
    applied = blurred + prior_term
    norm_now, curvature = lax.psum(
        (jnp.sum(residual * residual), jnp.sum(direction * applied)), ("chan", "facet")
    )
    step_size = norm_now / curvature
    new_solution = solution + step_size * direction
    new_residual = residual - step_size * applied
    norm_next = lax.psum(jnp.sum(new_residual * new_residual), ("chan", "facet"))
    new_direction = new_residual + norm_next / norm_now * direction
    return (new_solution, new_residual, new_direction)


def solution(mesh):
    return jax.shard_map(
        body,
        mesh=mesh,
        in_specs=(
            P("chan", "facet", None),
            P("chan", "facet", None),
            P("chan", "facet", None),
            P("chan", None, "facet"),
            P(),
            P(),
        ),
        out_specs=(P("chan", "facet", None), P("chan", "facet", None), P("chan", "facet", None)),
        check_vma=False,
    )
```

profile of v0, /device:TPU:0, one launch (start us, length us, event | category | flops | bytes accessed | tf_op | source)
XLA Modules:
  0.0 1117.8 jit_solution(16000557213750763182)
XLA Ops:
  0.6 10.9 copy.101
  11.5 7.3 all-to-all-start.2
  25.5 17.9 %convolution_bitcast_fusion.1 = f32[2,1,64,64,512]{4,2,3,0,1:T(8,128)S(1)} fusion(f32[512,32,64]{0,2,1:T(8,128)} %bitcast.178, f32[1,32,64]{2,1,0:T(8,128)S(1)} %get-tuple-element.34, f32[1,32,64]{2,1,0:T(8,128)S(1)} %get-tuple-element.35), kind=kOutput, calls=%fused_computation.36 | convolution fusion | flops 1610616832 | bytes 20987904 | tf_op jit(solution)/shard_map/grjn,qjk->qgknr/dot_general | solution.py:46
  50.3 12.1 %maximum_bitcast_fusion.2 = f32[2,64,64,512]{3,1,2,0:T(8,128)} fusion(f32[1,1,64,64,512]{4,2,3,0,1:T(8,128)} %get-tuple-element.23, f32[1,1,64,64,512]{4,2,3,0,1:T(8,128)} %get-tuple-element.22), kind=kLoop, calls=%fused_computation.12 | loop fusion | flops 4194304 | bytes 33554432 | tf_op jit(solution)/shard_map/reshape.11
  62.4 43.8 %fusion.21 = f32[2,64,64,512]{3,1,2,0:T(8,128)} fusion(f32[2,64,64,512]{3,1,2,0:T(8,128)} %maximum_bitcast_fusion.2, f32[1,2,64,64]{2,3,0,1:T(8,128)S(1)} %get-tuple-element.27, f32[1,2,64,64]{2,3,0,1:T(8,128)S(1)} %get-tuple-element.28), kind=kOutput, calls=%fused_computation.33 | convolution fusion | flops 6442467328 | bytes 33619968 | tf_op jit(solution)/shard_map/pgknr,pqnj->qgjkr/dot_general | solution.py:50
  106.2 15.3 %copy.83 = f32[2,64,64,512]{3,2,1,0:T(8,128)S(1)} copy(f32[2,64,64,512]{3,1,2,0:T(8,128)} %fusion.21) | data formatting | bytes 33554432 | tf_op jit(solution)/shard_map/pgknr,pqnj->qgjkr/dot_general | solution.py:50
  121.5 32.2 %copy.84 = f32[2,1,4096,512]{3,0,1,2:T(2,128)} copy(f32[2,1,4096,512]{3,2,0,1:T(8,128)S(1)} %bitcast.181) | data formatting | bytes 33554432 | tf_op jit(solution)/shard_map/reshape;pgknr,pqnj->qgjkr/transpose | solution.py:56
  160.7 17.8 %copy.90 = f32[64,64,1024]{2,0,1:T(8,128)} copy(f32[64,64,1024]{2,1,0:T(8,128)} %bitcast.185) | data formatting | bytes 33554432 | tf_op jit(solution)/shard_map/mul | solution.py:113
  204.3 139.5 %all-to-all-done = f32[2,1,4096,512]{3,0,1,2:T(2,128)} async-done(((f32[2,1,4096,512]{3,0,1,2:T(2,128)}), f32[2,1,4096,512]{3,0,1,2:T(2,128)}, u32[]{:S(2)}, u32[]{:S(2)}) %all-to-all-start) | async-done | bytes 16777248 | tf_op jit(solution)/shard_map/all_to_all | solution.py:111
  350.2 14.1 %copy.85 = f32[2,1,4096,512]{3,2,0,1:T(8,128)} copy(f32[2,1,4096,512]{3,0,1,2:T(2,128)} %all-to-all-done) | data formatting | bytes 33554432 | tf_op jit(solution)/shard_map/all_to_all | solution.py:111
  364.3 16.5 %copy.86 = f32[2,1,1024,4,512]{2,4,3,0,1:T(8,128)} copy(f32[2,1,1024,4,512]{4,2,3,0,1:T(8,128)} %bitcast.182) | data formatting | bytes 33554432 | tf_op jit(solution)/shard_map/all_to_all | solution.py:111
  380.8 43.3 %convolution_bitcast_fusion = f32[2,1,64,64,1024]{4,2,3,0,1:T(8,128)} fusion(f32[2,1024,32,64]{1,3,2,0:T(8,128)} %bitcast.179, f32[1,2,32,64]{3,2,1,0:T(8,128)S(1)} %get-tuple-element.33, f32[1,2,32,64]{3,2,1,0:T(8,128)S(1)} %get-tuple-element.32), kind=kOutput, calls=%fused_computation.11 | convolution fusion | flops 6442459136 | bytes 50364416 | tf_op jit(solution)/shard_map/pgcjn,pqjk->qgknc/dot_general | solution.py:63
  424.1 17.6 %multiply_subtract_fusion = (f32[1,1,64,64,1024]{4,2,3,0,1:T(8,128)S(1)}, f32[1,1,64,64,1024]{4,2,3,0,1:T(8,128)}) fusion(f32[2,1,64,64,1024]{4,2,3,0,1:T(8,128)} %convolution_bitcast_fusion, f32[64,64]{0,1:T(8,128)S(1)} %get-tuple-element.36, f32[64,64]{0,1:T(8,128)S(1)} %get-tuple-element.37), kind=kLoop, calls=%fused_computation.28 | loop fusion | flops 25165824 | bytes 67141632 | tf_op jit(solution)/shard_map/sub | solution.py:38
  441.7 19.0 %maximum_bitcast_fusion = f32[2,64,64,1024,1]{3,1,2,0,4:T(8,128)} fusion(f32[1,1,64,64,1024]{4,2,3,0,1:T(8,128)} %get-tuple-element.19, f32[1,1,64,64,1024]{4,2,3,0,1:T(8,128)S(1)} %get-tuple-element.18), kind=kLoop, calls=%fused_computation | loop fusion | flops 8388608 | bytes 67108864 | tf_op jit(solution)/shard_map/reshape.24
  460.8 58.6 %fusion.4 = f32[2,64,64,1024,1]{3,1,4,0,2:T(8,128)} fusion(f32[2,64,64,1024,1]{3,1,2,0,4:T(8,128)} %maximum_bitcast_fusion, f32[1,2,64,64]{2,3,0,1:T(8,128)S(1)} %get-tuple-element.27, f32[1,2,64,64]{2,3,0,1:T(8,128)S(1)} %get-tuple-element.28), kind=kOutput, calls=%fused_computation.7 | convolution fusion | flops 12884918272 | bytes 67174400 | tf_op jit(solution)/shard_map/pgknc,pqnj->qgjkc/dot_general | solution.py:67
  519.3 38.5 %fusion.7 = f32[2,64,64,1024]{3,1,2,0:T(8,128)} fusion(f32[2,64,64,1024,1]{3,1,4,0,2:T(8,128)} %fusion.4, f32[64,64,1024]{2,0,1:T(8,128)} %copy.90, f32[1,2,64,64]{2,3,1,0:T(8,128)S(1)} %copy-done.6, f32[1,2,64,64]{2,3,1,0:T(8,128)S(1)} %copy-done.5), kind=kOutput, calls=%fused_computation.10 | convolution fusion | flops 12893306880 | bytes 83951616 | tf_op jit(solution)/shard_map/pgjkc,pqjn->qgnkc/dot_general | solution.py:80
  557.9 17.7 %subtract_bitcast_fusion = (f32[1,1,64,64,1024]{4,2,3,1,0:T(8,128)S(1)}, f32[1,1,64,64,1024]{4,2,3,1,0:T(8,128)}) fusion(f32[2,64,64,1024]{3,1,2,0:T(8,128)} %fusion.7, f32[64,64]{0,1:T(8,128)S(1)} %fusion.73, f32[64,64]{0,1:T(8,128)S(1)} %get-tuple-element.37), kind=kLoop, calls=%fused_computation.25 | loop fusion | flops 25165824 | bytes 67141632 | tf_op jit(solution)/shard_map/stack | solution.py:37
  575.5 18.8 %maximum_bitcast_fusion.1 = f32[2,64,64,1024]{3,1,2,0:T(8,128)} fusion(f32[1,1,64,64,1024]{4,2,3,1,0:T(8,128)} %get-tuple-element.17, f32[1,1,64,64,1024]{4,2,3,1,0:T(8,128)S(1)} %get-tuple-element.16), kind=kLoop, calls=%fused_computation.1 | loop fusion | flops 8388608 | bytes 67108864 | tf_op jit(solution)/shard_map/reshape.38
  594.3 51.4 %fusion.27 = f32[2,32,64,1024]{3,1,2,0:T(8,128)S(1)} fusion(f32[2,64,64,1024]{3,1,2,0:T(8,128)} %maximum_bitcast_fusion.1, f32[1,2,64,32]{2,3,0,1:T(8,128)S(1)} %copy-done.12, f32[1,2,64,32]{2,3,0,1:T(8,128)S(1)} %copy-done.11), kind=kOutput, calls=%fused_computation.35 | convolution fusion | flops 6442459136 | bytes 50364416 | tf_op jit(solution)/shard_map/pgnkc,pqkj->qgjnc/dot_general | solution.py:84
  645.8 19.4 %copy.93 = f32[2,32,64,1024]{3,2,1,0:T(8,128)} copy(f32[2,32,64,1024]{3,1,2,0:T(8,128)S(1)} %fusion.27) | data formatting | bytes 33554432 | tf_op jit(solution)/shard_map/pgnkc,pqkj->qgjnc/dot_general | solution.py:84
  665.2 28.6 %copy.94 = f32[2,1,2048,1024]{3,0,1,2:T(2,128)} copy(f32[2,1,2048,1024]{3,2,0,1:T(8,128)} %bitcast.183) | data formatting | bytes 33554432 | tf_op jit(solution)/shard_map/reshape;pgnkc,pqkj->qgjnc/transpose | solution.py:90
  715.4 168.4 %all-to-all-done.1 = f32[2,1,2048,1024]{3,0,1,2:T(2,128)} async-done(((f32[2,1,2048,1024]{3,0,1,2:T(2,128)}), f32[2,1,2048,1024]{3,0,1,2:T(2,128)}, u32[]{:S(2)}, u32[]{:S(2)}) %all-to-all-start.1) | async-done | bytes 16777248 | tf_op jit(solution)/shard_map/all_to_all | solution.py:115
  883.8 15.8 %copy.95 = f32[2,1,2048,1024]{3,2,0,1:T(8,128)} copy(f32[2,1,2048,1024]{3,0,1,2:T(2,128)} %all-to-all-done.1) | data formatting | bytes 33554432 | tf_op jit(solution)/shard_map/all_to_all | solution.py:115
  899.6 16.4 %copy.96 = f32[2,1,512,4,1024]{2,4,3,0,1:T(8,128)} copy(f32[2,1,512,4,1024]{4,2,3,0,1:T(8,128)} %bitcast.184) | data formatting | bytes 33554432 | tf_op jit(solution)/shard_map/all_to_all | solution.py:115
  916.1 33.0 %fusion.24 = f32[2,1,64,64,512]{4,2,3,0,1:T(8,128)} fusion(f32[2,512,64,64]{1,3,2,0:T(8,128)} %bitcast.180, f32[1,2,64,64]{2,3,1,0:T(8,128)S(1)} %copy-done.6, f32[1,2,64,64]{2,3,1,0:T(8,128)S(1)} %copy-done.5), kind=kOutput, calls=%fused_computation.34 | convolution fusion | flops 6442467328 | bytes 33619968 | tf_op jit(solution)/shard_map/pgrjk,pqjn->qgnkr/dot_general | solution.py:97
  949.1 10.9 multiply_subtract_fusion.1
  960.0 7.4 maximum_bitcast_fusion.3
  967.5 18.7 %fusion.33 = f32[1,512,32,64]{1,2,3,0:T(8,128)S(1)} fusion(f32[2,64,64,512]{3,1,2,0:T(8,128)S(1)} %maximum_bitcast_fusion.3, f32[1,64,32]{1,2,0:T(8,128)S(1)} %copy-done.10, f32[1,64,32]{1,2,0:T(8,128)S(1)} %copy-done.8), kind=kOutput, calls=%fused_computation.43 | convolution fusion | flops 1611665408 | bytes 20987904 | tf_op jit(solution)/shard_map/pgnkr,pkj->grjn/dot_general | solution.py:103
  998.1 40.3 %all-reduce = (f32[]{:T(128)}, f32[]{:T(128)}) all-reduce(f32[]{:T(128)} %multiply_reduce_fusion.2, f32[]{:T(128)} %multiply_reduce_fusion.1), channel_id=1, replica_groups=mesh['chan'=8,'facet'=4] {'chan','facet'}, use_global_device_ids=true, to_apply=%region_1.2 | all-reduce | flops 2 | bytes 16 | tf_op jit(solution)/shard_map/psum | solution.py:128
  1039.7 9.2 multiply_reduce_fusion
  1048.9 41.4 %psum.23 = f32[]{:T(128)} all-reduce(f32[]{:T(128)} %get-tuple-element.14), channel_id=1, replica_groups=mesh['chan'=8,'facet'=4] {'chan','facet'}, use_global_device_ids=true, to_apply=%region_5.6 | all-reduce | flops 1 | bytes 8 | tf_op jit(solution)/shard_map/psum | solution.py:134
  1097.0 9.6 multiply_add_fusion.3
  (62 shorter events, 102.2 us)
Async XLA Ops:
  0.6 178.9 %copy-start = (f32[8,8]{1,0:T(8,128)S(1)}, f32[8,8]{1,0:T(8,128)}, u32[]{:S(2)}) copy-start(f32[8,8]{1,0:T(8,128)} %param.10) | copy-start | bytes 772
  11.5 142.2 %all-to-all-start.2 = ((f32[1,512,2048]{1,0,2:T(1,128)}), f32[1,512,2048]{1,0,2:T(1,128)}, u32[]{:S(2)}, u32[]{:S(2)}) async-start(f32[1,512,2048]{1,0,2:T(1,128)} %copy.101), calls=%async_computation.2 | async-start | bytes 8388608 | tf_op jit(solution)/shard_map/all_to_all | solution.py:117
  153.8 190.0 %all-to-all-start = ((f32[2,1,4096,512]{3,0,1,2:T(2,128)}), f32[2,1,4096,512]{3,0,1,2:T(2,128)}, u32[]{:S(2)}, u32[]{:S(2)}) async-start(f32[2,1,4096,512]{3,0,1,2:T(2,128)} %copy.84), calls=%async_computation | async-start | bytes 33554432 | tf_op jit(solution)/shard_map/all_to_all | solution.py:111
  160.7 18.8 %copy-start.13 = (s32[8]{0:T(128)S(1)}, s32[8]{0:T(128)}, u32[]{:S(2)}) copy-start(s32[8]{0:T(128)} %param.11) | copy-start | bytes 100
  178.7 22.3 %copy-start.7 = (f32[1,64,32]{1,2,0:T(8,128)}, f32[1,64,32]{1,2,0:T(8,128)S(1)}, u32[]{:S(2)}) copy-start(f32[1,64,32]{1,2,0:T(8,128)S(1)} %fusion.88) | copy-start | bytes 24580
  178.9 22.0 %copy-start.9 = (f32[1,64,32]{1,2,0:T(8,128)}, f32[1,64,32]{1,2,0:T(8,128)S(1)}, u32[]{:S(2)}) copy-start(f32[1,64,32]{1,2,0:T(8,128)S(1)} %get-tuple-element.43) | copy-start | bytes 24580
  343.8 350.0 %all-to-all-start.3 = ((f32[8,512,256]{2,1,0:T(8,128)}), f32[8,512,256]{2,1,0:T(8,128)}, u32[]{:S(2)}, u32[]{:S(2)}) async-start(f32[8,512,256]{2,1,0:T(8,128)} %copy.104), calls=%async_computation.3 | async-start | bytes 8388608 | tf_op jit(solution)/shard_map/all_to_all | solution.py:126
  460.8 58.6 %copy-start.5 = (f32[1,2,64,64]{2,3,1,0:T(8,128)S(1)}, f32[1,2,64,64]{2,3,1,0:T(8,128)}, u32[]{:S(2)}) copy-start(f32[1,2,64,64]{2,3,1,0:T(8,128)} %get-tuple-element.26) | copy-start | bytes 98308
  460.8 58.6 %copy-start.6 = (f32[1,2,64,64]{2,3,1,0:T(8,128)S(1)}, f32[1,2,64,64]{2,3,1,0:T(8,128)}, u32[]{:S(2)}) copy-start(f32[1,2,64,64]{2,3,1,0:T(8,128)} %get-tuple-element.29) | copy-start | bytes 98308
  575.5 18.8 %copy-start.11 = (f32[1,2,64,32]{2,3,0,1:T(8,128)S(1)}, f32[1,2,64,32]{2,3,0,1:T(8,128)}, u32[]{:S(2)}) copy-start(f32[1,2,64,32]{2,3,0,1:T(8,128)} %get-tuple-element.30) | copy-start | bytes 49156
  575.5 18.8 %copy-start.12 = (f32[1,2,64,32]{2,3,0,1:T(8,128)S(1)}, f32[1,2,64,32]{2,3,0,1:T(8,128)}, u32[]{:S(2)}) copy-start(f32[1,2,64,32]{2,3,0,1:T(8,128)} %get-tuple-element.31) | copy-start | bytes 49156
  693.8 190.0 %all-to-all-start.1 = ((f32[2,1,2048,1024]{3,0,1,2:T(2,128)}), f32[2,1,2048,1024]{3,0,1,2:T(2,128)}, u32[]{:S(2)}, u32[]{:S(2)}) async-start(f32[2,1,2048,1024]{3,0,1,2:T(2,128)} %copy.94), calls=%async_computation.1 | async-start | bytes 33554432 | tf_op jit(solution)/shard_map/all_to_all | solution.py:115
  960.0 7.4 copy-start.8
  960.0 7.4 copy-start.10
  967.4 23.2 %copy-start.2 = (f32[1,512,2048]{1,2,0:T(8,128)S(1)}, f32[1,512,2048]{1,2,0:T(8,128)}, u32[]{:S(2)}) copy-start(f32[1,512,2048]{1,2,0:T(8,128)} %copy.106) | copy-start | bytes 12582916
  967.5 23.2 %copy-start.3 = (f32[1,512,8,256]{1,3,2,0:T(8,128)S(1)}, f32[1,512,8,256]{1,3,2,0:T(8,128)}, u32[]{:S(2)}) copy-start(f32[1,512,8,256]{1,3,2,0:T(8,128)} %copy.105) | copy-start | bytes 12582916
  988.6 2.0 copy-start.4
  1091.7 25.7 %copy-start.1 = (f32[8,8]{1,0:T(8,128)S(1)}, f32[8,8]{1,0:T(8,128)}, u32[]{:S(2)}) copy-start(f32[8,8]{1,0:T(8,128)} %param.10) | copy-start | bytes 772
where the time goes:
time: 1130 us; the launch traced here: 1120 us
  matrix products  317 us (28%)
  waiting for transfers between devices  308 us (27%)
  local copies, waits for them, and re-layouts  242 us (21%)
  other arithmetic  138 us (12%)
  blocking collectives  81.7 us (7%)
  starting transfers between devices  27.7 us (2%)
    all_to_all x1, waiting for transfers between devices, body(): lax.all_to_all(inverted, 'facet', split_axis=2, concat_axis=3, tiled=True)  168 us
    all_to_all x1, waiting for transfers between devices, body(): lax.all_to_all(columns, 'facet', split_axis=2, concat_axis=3, tiled=True)  140 us
    dot_general x1, matrix products, forward_rows(): jnp.einsum('pgknc,pqnj->qgjkc', section_one, complex_table(factor, factor...  58.6 us
    another operation x4, other arithmetic  57.3 us
    dot_general x1, matrix products, inverse_rows(): jnp.einsum('pgnkc,pqkj->qgjnc', section_one, complex_table(factor, halved...  51.4 us
    unnamed x36, local copies, waits for them, and re-layouts  49.6 us
    dot_general x1, matrix products, forward_columns(): jnp.einsum('pgknr,pqnj->qgjkr', section_one, complex_table(factor, factor...  43.8 us
    dot_general x1, matrix products, forward_rows(): jnp.einsum('pgcjn,pqjk->qgknc', blocks, complex_table(halved, factor, fac...  43.3 us
  transfers between devices with their start and end apart: 4, of which 2 were waited for; matrix products, arithmetic and copies ran while one was open for 48% of the time, Pallas kernels for 0%

commit v1 on v0

--- a/solution.py
+++ b/solution.py
@@ -7,6 +7,22 @@
 ROOT = 64
 HIGHEST = lax.Precision.HIGHEST
 PRIOR_FLOOR = 0.25
+
+
+def swapped_with_each(x, axis, split, join):
+    ways, here = (lax.axis_size(axis), lax.axis_index(axis))
+    width = x.shape[split] // ways
+    lengths = list(x.shape)
+    lengths[split] = width
+    height = lengths[join]
+    lengths[join] = height * ways
+    full = jnp.zeros(lengths, x.dtype)
+    for mask in range(ways):
+        part = lax.dynamic_slice_in_dim(x, (here ^ mask) * width, width, axis=split)
+        if mask:
+            part = lax.ppermute(part, axis, [(d, d ^ mask) for d in range(ways)])
+        full = lax.dynamic_update_slice_in_dim(full, part, (here ^ mask) * height, axis=join)
+    return full
 
 
 def twiddle_table(left_size, right_size, length, direction_sign):
@@ -108,7 +124,7 @@
 def body(solution, residual, direction, spectra, basis, slot_channel):
     channel_count = basis.shape[0]
     columns = forward_columns(direction, ROOT)
-    swapped = lax.all_to_all(columns, "facet", split_axis=2, concat_axis=3, tiled=True)
+    swapped = swapped_with_each(columns, "facet", 2, 3)
     row_spectra = forward_rows(swapped, ROOT)
     weighted = row_spectra * spectra[None]
     inverted = inverse_rows(weighted, ROOT)

time: 1130 us -> 1080 us (0.956)
  waiting for transfers between devices: 308 us -> 278 us
    all_to_all x1 -> x0, waiting for transfers between devices: 140 us -> none  [body(): lax.all_to_all(columns, 'facet', split_axis=2, concat_axis=3, tiled=True)]
    ppermute x0 -> x3, waiting for transfers between devices: none -> 109 us  [swapped_with_each(): part = lax.ppermute(part, axis, [(d, d ^ mask) for d in range(ways)])]
    transpose x1 -> x0, local copies, waits for them, and re-layouts: 32.2 us -> none  [forward_columns(): return second.reshape(2, groups, factor * factor, height)]
    all_to_all x2 -> x0, local copies, waits for them, and re-layouts: 30.6 us -> none  [body(): lax.all_to_all(columns, 'facet', split_axis=2, concat_axis=3, tiled=True)]
    dynamic_slice x0 -> x2, local copies, waits for them, and re-layouts: none -> 17.8 us  [swapped_with_each(): part = lax.dynamic_slice_in_dim(x, (here ^ mask) * width, width, axis=split)]
    dynamic_update_slice x0 -> x4, local copies, waits for them, and re-layouts: none -> 16.5 us  [swapped_with_each(): lax.dynamic_update_slice_in_dim(full, part, (here ^ mask) * height, axis=...]
    ppermute x0 -> x3, local copies, waits for them, and re-layouts: none -> 16.2 us  [swapped_with_each(): part = lax.ppermute(part, axis, [(d, d ^ mask) for d in range(ways)])]
    unnamed x36 -> x38, local copies, waits for them, and re-layouts: 49.6 us -> 49.7 us
  transfers between devices with their start and end apart: 4 -> 6, of which waited for: 2 -> 3; matrix products, arithmetic and copies ran while one was open for 48% -> 38% of each run, Pallas kernels for 0% -> 0%
where the time goes in v1:
time: 1080 us; the launch traced here: 1070 us
  matrix products  307 us (28%)
  waiting for transfers between devices  278 us (26%)
  local copies, waits for them, and re-layouts  240 us (22%)
  other arithmetic  138 us (13%)
  blocking collectives  81.7 us (8%)
  starting transfers between devices  22 us (2%)
    all_to_all x1, waiting for transfers between devices, body(): lax.all_to_all(inverted, 'facet', split_axis=2, concat_axis=3, tiled=True)  168 us
    ppermute x3, waiting for transfers between devices, swapped_with_each(): part = lax.ppermute(part, axis, [(d, d ^ mask) for d in range(ways)])  109 us
    dot_general x1, matrix products, forward_rows(): jnp.einsum('pgknc,pqnj->qgjkc', section_one, complex_table(factor, factor...  58.8 us
    another operation x4, other arithmetic  57.6 us
    dot_general x1, matrix products, inverse_rows(): jnp.einsum('pgnkc,pqkj->qgjnc', section_one, complex_table(factor, halved...  51.4 us
    unnamed x38, local copies, waits for them, and re-layouts  49.7 us
    dot_general x1, matrix products, forward_rows(): jnp.einsum('pgcjn,pqjk->qgknc', blocks, complex_table(halved, factor, fac...  43.6 us
    psum x1, blocking collectives, body(): lax.psum(jnp.sum(new_residual * new_residual), ('chan', 'facet'))  41.4 us
  transfers between devices with their start and end apart: 6, of which 3 were waited for; matrix products, arithmetic and copies ran while one was open for 38% of the time, Pallas kernels for 0%

profile of v1, /device:TPU:0, one launch (start us, length us, event | category | flops | bytes accessed | tf_op | source)
XLA Modules:
  0.0 1070.5 jit_solution(7363310896771513146)
XLA Ops:
  6.7 17.9 %convolution_bitcast_fusion.1 = f32[2,1,64,64,512]{4,2,3,0,1:T(8,128)S(1)} fusion(f32[512,32,64]{0,2,1:T(8,128)} %bitcast.175, f32[1,32,64]{2,1,0:T(8,128)S(1)} %get-tuple-element.38, f32[1,32,64]{2,1,0:T(8,128)S(1)} %get-tuple-element.39), kind=kOutput, calls=%fused_computation.36 | convolution fusion | flops 1610616832 | bytes 20987904 | tf_op jit(solution)/shard_map/grjn,qjk->qgknr/dot_general | solution.py:62
  31.4 12.1 %maximum_bitcast_fusion.2 = f32[2,64,64,512]{3,1,2,0:T(8,128)} fusion(f32[1,1,64,64,512]{4,2,3,0,1:T(8,128)} %get-tuple-element.23, f32[1,1,64,64,512]{4,2,3,0,1:T(8,128)} %get-tuple-element.22), kind=kLoop, calls=%fused_computation.12 | loop fusion | flops 4194304 | bytes 33554432 | tf_op jit(solution)/shard_map/reshape.11
  44.2 33.2 %fusion.21 = f32[2,64,64,512]{3,1,2,0:T(8,128)} fusion(f32[2,64,64,512]{3,1,2,0:T(8,128)} %maximum_bitcast_fusion.2, f32[1,2,64,64]{2,3,0,1:T(8,128)S(1)} %get-tuple-element.31, f32[1,2,64,64]{2,3,0,1:T(8,128)S(1)} %get-tuple-element.32), kind=kOutput, calls=%fused_computation.33 | convolution fusion | flops 6442467328 | bytes 33619968 | tf_op jit(solution)/shard_map/pgknr,pqnj->qgjkr/dot_general | solution.py:66
  77.4 17.7 %copy.89 = f32[2,64,64,512]{3,2,1,0:T(8,128)} copy(f32[2,64,64,512]{3,1,2,0:T(8,128)} %fusion.21) | data formatting | bytes 33554432 | tf_op jit(solution)/shard_map/pgknr,pqnj->qgjkr/dot_general | solution.py:66
  95.2 12.4 %constant_dynamic-slice_fusion = (f32[2,1,1024,512]{3,2,0,1:T(8,128)}, f32[2,1,1024,512]{3,2,0,1:T(8,128)}, f32[2,1,1024,512]{3,2,0,1:T(8,128)}, f32[2,1,1024,512]{3,2,0,1:T(8,128)}) fusion(f32[2,1,4096,512]{3,2,0,1:T(8,128)} %bitcast.176, s32[]{:T(128)S(6)} %select_n.196, s32[]{:T(128)S(6)} %select_n.194, s32[]{:T(128)S(6)} %select_n.192, s32[]{:T(128)S(6)} %select_n.190), kind=kLoop, calls=%fused_computation.135 | loop fusion | bytes 33554448 | tf_op jit(solution)/shard_map/dynamic_slice | solution.py:21
  110.7 10.9 %copy.108 = f32[1,512,2048]{1,0,2:T(1,128)} copy(f32[1,512,2048]{2,1,0:T(8,128)} %param.8) | data formatting | bytes 8388608 | tf_op args[2]
  133.0 17.7 %copy.97 = f32[64,64,1024]{2,0,1:T(8,128)} copy(f32[64,64,1024]{2,1,0:T(8,128)} %bitcast.180) | data formatting | bytes 33554432 | tf_op jit(solution)/shard_map/mul | solution.py:129
  152.0 7.9 broadcast_in_dim.2
  167.6 34.7 %collective-permute-done.1 = f32[2,1,1024,512]{3,2,0,1:T(8,128)} collective-permute-done((f32[2,1,1024,512]{3,2,0,1:T(8,128)}, f32[2,1,1024,512]{3,2,0,1:T(8,128)}, u32[]{:S(2)}, u32[]{:S(2)}) %collective-permute-start.1) | collective-permute-done | bytes 4194336 | tf_op jit(solution)/shard_map/ppermute | solution.py:23
  217.2 74.5 %collective-permute-done.2 = f32[2,1,1024,512]{3,2,0,1:T(8,128)} collective-permute-done((f32[2,1,1024,512]{3,2,0,1:T(8,128)}, f32[2,1,1024,512]{3,2,0,1:T(8,128)}, u32[]{:S(2)}, u32[]{:S(2)}) %collective-permute-start.2) | collective-permute-done | bytes 4194336 | tf_op jit(solution)/shard_map/ppermute | solution.py:23
  301.9 43.6 %convolution_bitcast_fusion = f32[2,1,64,64,1024]{4,2,3,0,1:T(8,128)} fusion(f32[2,1024,32,64]{1,3,2,0:T(8,128)} %bitcast.30, f32[1,2,32,64]{3,2,1,0:T(8,128)S(1)} %get-tuple-element.37, f32[1,2,32,64]{3,2,1,0:T(8,128)S(1)} %get-tuple-element.36), kind=kOutput, calls=%fused_computation.11 | convolution fusion | flops 6442459136 | bytes 50364416 | tf_op jit(solution)/shard_map/pgcjn,pqjk->qgknc/dot_general | solution.py:79
  345.4 17.7 %multiply_subtract_fusion = (f32[1,1,64,64,1024]{4,2,3,0,1:T(8,128)S(1)}, f32[1,1,64,64,1024]{4,2,3,0,1:T(8,128)}) fusion(f32[2,1,64,64,1024]{4,2,3,0,1:T(8,128)} %convolution_bitcast_fusion, f32[64,64]{0,1:T(8,128)S(1)} %get-tuple-element.40, f32[64,64]{0,1:T(8,128)S(1)} %get-tuple-element.41), kind=kLoop, calls=%fused_computation.28 | loop fusion | flops 25165824 | bytes 67141632 | tf_op jit(solution)/shard_map/sub | solution.py:54
  363.2 19.1 %maximum_bitcast_fusion = f32[2,64,64,1024,1]{3,1,2,0,4:T(8,128)} fusion(f32[1,1,64,64,1024]{4,2,3,0,1:T(8,128)} %get-tuple-element.19, f32[1,1,64,64,1024]{4,2,3,0,1:T(8,128)S(1)} %get-tuple-element.18), kind=kLoop, calls=%fused_computation | loop fusion | flops 8388608 | bytes 67108864 | tf_op jit(solution)/shard_map/reshape.23
  382.2 58.8 %fusion.4 = f32[2,64,64,1024,1]{3,1,4,0,2:T(8,128)} fusion(f32[2,64,64,1024,1]{3,1,2,0,4:T(8,128)} %maximum_bitcast_fusion, f32[1,2,64,64]{2,3,0,1:T(8,128)S(1)} %get-tuple-element.31, f32[1,2,64,64]{2,3,0,1:T(8,128)S(1)} %get-tuple-element.32), kind=kOutput, calls=%fused_computation.7 | convolution fusion | flops 12884918272 | bytes 67174400 | tf_op jit(solution)/shard_map/pgknc,pqnj->qgjkc/dot_general | solution.py:83
  471.4 38.6 %fusion.7 = f32[2,64,64,1024]{3,1,2,0:T(8,128)} fusion(f32[2,64,64,1024,1]{3,1,4,0,2:T(8,128)} %fusion.4, f32[64,64,1024]{2,0,1:T(8,128)} %copy.97, f32[1,2,64,64]{2,3,1,0:T(8,128)S(1)} %copy-done.7, f32[1,2,64,64]{2,3,1,0:T(8,128)S(1)} %copy-done.6), kind=kOutput, calls=%fused_computation.10 | convolution fusion | flops 12893306880 | bytes 83951616 | tf_op jit(solution)/shard_map/pgjkc,pqjn->qgnkc/dot_general | solution.py:96
  510.0 17.6 %subtract_bitcast_fusion = (f32[1,1,64,64,1024]{4,2,3,1,0:T(8,128)S(1)}, f32[1,1,64,64,1024]{4,2,3,1,0:T(8,128)}) fusion(f32[2,64,64,1024]{3,1,2,0:T(8,128)} %fusion.7, f32[64,64]{0,1:T(8,128)S(1)} %fusion.73, f32[64,64]{0,1:T(8,128)S(1)} %get-tuple-element.41), kind=kLoop, calls=%fused_computation.25 | loop fusion | flops 25165824 | bytes 67141632 | tf_op jit(solution)/shard_map/stack | solution.py:53
  527.6 19.1 %maximum_bitcast_fusion.1 = f32[2,64,64,1024]{3,1,2,0:T(8,128)} fusion(f32[1,1,64,64,1024]{4,2,3,1,0:T(8,128)} %get-tuple-element.17, f32[1,1,64,64,1024]{4,2,3,1,0:T(8,128)S(1)} %get-tuple-element.16), kind=kLoop, calls=%fused_computation.1 | loop fusion | flops 8388608 | bytes 67108864 | tf_op jit(solution)/shard_map/reshape.37
  546.6 51.4 %fusion.27 = f32[2,32,64,1024]{3,1,2,0:T(8,128)S(1)} fusion(f32[2,64,64,1024]{3,1,2,0:T(8,128)} %maximum_bitcast_fusion.1, f32[1,2,64,32]{2,3,0,1:T(8,128)S(1)} %copy-done.13, f32[1,2,64,32]{2,3,0,1:T(8,128)S(1)} %copy-done.12), kind=kOutput, calls=%fused_computation.35 | convolution fusion | flops 6442459136 | bytes 50364416 | tf_op jit(solution)/shard_map/pgnkc,pqkj->qgjnc/dot_general | solution.py:100
  598.1 19.4 %copy.100 = f32[2,32,64,1024]{3,2,1,0:T(8,128)} copy(f32[2,32,64,1024]{3,1,2,0:T(8,128)S(1)} %fusion.27) | data formatting | bytes 33554432 | tf_op jit(solution)/shard_map/pgnkc,pqkj->qgjnc/dot_general | solution.py:100
  617.5 28.6 %copy.101 = f32[2,1,2048,1024]{3,0,1,2:T(2,128)} copy(f32[2,1,2048,1024]{3,2,0,1:T(8,128)} %bitcast.178) | data formatting | bytes 33554432 | tf_op jit(solution)/shard_map/reshape;pgnkc,pqkj->qgjnc/transpose | solution.py:106
  646.1 7.0 all-to-all-start
  667.7 168.4 %all-to-all-done = f32[2,1,2048,1024]{3,0,1,2:T(2,128)} async-done(((f32[2,1,2048,1024]{3,0,1,2:T(2,128)}), f32[2,1,2048,1024]{3,0,1,2:T(2,128)}, u32[]{:S(2)}, u32[]{:S(2)}) %all-to-all-start) | async-done | bytes 16777248 | tf_op jit(solution)/shard_map/all_to_all | solution.py:131
  836.1 15.8 %copy.102 = f32[2,1,2048,1024]{3,2,0,1:T(8,128)} copy(f32[2,1,2048,1024]{3,0,1,2:T(2,128)} %all-to-all-done) | data formatting | bytes 33554432 | tf_op jit(solution)/shard_map/all_to_all | solution.py:131
  852.0 16.5 %copy.103 = f32[2,1,512,4,1024]{2,4,3,0,1:T(8,128)} copy(f32[2,1,512,4,1024]{4,2,3,0,1:T(8,128)} %bitcast.179) | data formatting | bytes 33554432 | tf_op jit(solution)/shard_map/all_to_all | solution.py:131
  868.4 33.0 %fusion.24 = f32[2,1,64,64,512]{4,2,3,0,1:T(8,128)} fusion(f32[2,512,64,64]{1,3,2,0:T(8,128)} %bitcast.177, f32[1,2,64,64]{2,3,1,0:T(8,128)S(1)} %copy-done.7, f32[1,2,64,64]{2,3,1,0:T(8,128)S(1)} %copy-done.6), kind=kOutput, calls=%fused_computation.34 | convolution fusion | flops 6442467328 | bytes 33619968 | tf_op jit(solution)/shard_map/pgrjk,pqjn->qgnkr/dot_general | solution.py:113
  901.5 10.9 %multiply_subtract_fusion.1 = (f32[1,1,64,64,512]{4,2,3,0,1:T(8,128)}, f32[1,1,64,64,512]{4,2,3,0,1:T(8,128)}) fusion(f32[2,1,64,64,512]{4,2,3,0,1:T(8,128)} %fusion.24, f32[64,64]{0,1:T(8,128)S(1)} %fusion.73, f32[64,64]{0,1:T(8,128)S(1)} %get-tuple-element.41), kind=kLoop, calls=%fused_computation.30 | loop fusion | flops 12582912 | bytes 33587200 | tf_op jit(solution)/shard_map/sub | solution.py:54
  912.4 7.4 maximum_bitcast_fusion.3
  919.8 18.7 %fusion.33 = f32[1,512,32,64]{1,2,3,0:T(8,128)S(1)} fusion(f32[2,64,64,512]{3,1,2,0:T(8,128)S(1)} %maximum_bitcast_fusion.3, f32[1,64,32]{1,2,0:T(8,128)S(1)} %copy-done.11, f32[1,64,32]{1,2,0:T(8,128)S(1)} %copy-done.9), kind=kOutput, calls=%fused_computation.43 | convolution fusion | flops 1611665408 | bytes 20987904 | tf_op jit(solution)/shard_map/pgnkr,pkj->grjn/dot_general | solution.py:119
  950.6 40.3 %all-reduce = (f32[]{:T(128)}, f32[]{:T(128)}) all-reduce(f32[]{:T(128)} %multiply_reduce_fusion.2, f32[]{:T(128)} %multiply_reduce_fusion.1), channel_id=1, replica_groups=mesh['chan'=8,'facet'=4] {'chan','facet'}, use_global_device_ids=true, to_apply=%region_1.2 | all-reduce | flops 2 | bytes 16 | tf_op jit(solution)/shard_map/psum | solution.py:144
  992.3 9.3 multiply_reduce_fusion
  1001.6 41.4 %psum.23 = f32[]{:T(128)} all-reduce(f32[]{:T(128)} %get-tuple-element.14), channel_id=1, replica_groups=mesh['chan'=8,'facet'=4] {'chan','facet'}, use_global_device_ids=true, to_apply=%region_5.6 | all-reduce | flops 1 | bytes 8 | tf_op jit(solution)/shard_map/psum | solution.py:150
  1049.8 9.6 multiply_add_fusion.3
  (75 shorter events, 135.0 us)
Async XLA Ops:
  0.6 151.2 %copy-start = (f32[8,8]{1,0:T(8,128)S(1)}, f32[8,8]{1,0:T(8,128)}, u32[]{:S(2)}) copy-start(f32[8,8]{1,0:T(8,128)} %param.10) | copy-start | bytes 772
  107.6 54.6 %collective-permute-start = (f32[2,1,1024,512]{3,2,0,1:T(8,128)}, f32[2,1,1024,512]{3,2,0,1:T(8,128)}, u32[]{:S(2)}, u32[]{:S(2)}) collective-permute-start(f32[2,1,1024,512]{3,2,0,1:T(8,128)} %get-tuple-element.26), channel_id=1, source_target_pairs={{0,1},{1,0},{2,3},{3,2},{4,5},{5,4},{6,7},{7,6},{8,9},{9,8},{10,11... | collective-permute-start | bytes 12582920 | tf_op jit(solution)/shard_map/ppermute | solution.py:23
  108.1 94.3 %collective-permute-start.1 = (f32[2,1,1024,512]{3,2,0,1:T(8,128)}, f32[2,1,1024,512]{3,2,0,1:T(8,128)}, u32[]{:S(2)}, u32[]{:S(2)}) collective-permute-start(f32[2,1,1024,512]{3,2,0,1:T(8,128)} %get-tuple-element.25), channel_id=1, source_target_pairs={{0,2},{1,3},{2,0},{3,1},{4,6},{5,7},{6,4},{7,5},{8,10},{9,11},{10,... | collective-permute-start | bytes 12582920 | tf_op jit(solution)/shard_map/ppermute | solution.py:23
  110.6 181.1 %collective-permute-start.2 = (f32[2,1,1024,512]{3,2,0,1:T(8,128)}, f32[2,1,1024,512]{3,2,0,1:T(8,128)}, u32[]{:S(2)}, u32[]{:S(2)}) collective-permute-start(f32[2,1,1024,512]{3,2,0,1:T(8,128)} %get-tuple-element.24), channel_id=1, source_target_pairs={{0,3},{1,2},{2,1},{3,0},{4,7},{5,6},{6,5},{7,4},{8,11},{9,10},{10,... | collective-permute-start | bytes 12582920 | tf_op jit(solution)/shard_map/ppermute | solution.py:23
  121.5 319.5 %all-to-all-start.1 = ((f32[1,512,2048]{1,0,2:T(1,128)}), f32[1,512,2048]{1,0,2:T(1,128)}, u32[]{:S(2)}, u32[]{:S(2)}) async-start(f32[1,512,2048]{1,0,2:T(1,128)} %copy.108), calls=%async_computation.1 | async-start | bytes 8388608 | tf_op jit(solution)/shard_map/all_to_all | solution.py:133
  133.0 18.8 %copy-start.14 = (s32[8]{0:T(128)S(1)}, s32[8]{0:T(128)}, u32[]{:S(2)}) copy-start(s32[8]{0:T(128)} %param.11) | copy-start | bytes 100
  150.7 9.2 copy-start.5
  150.9 11.3 %copy-start.8 = (f32[1,64,32]{1,2,0:T(8,128)}, f32[1,64,32]{1,2,0:T(8,128)S(1)}, u32[]{:S(2)}) copy-start(f32[1,64,32]{1,2,0:T(8,128)S(1)} %fusion.88) | copy-start | bytes 24580
  151.1 11.1 %copy-start.10 = (f32[1,64,32]{1,2,0:T(8,128)}, f32[1,64,32]{1,2,0:T(8,128)S(1)}, u32[]{:S(2)}) copy-start(f32[1,64,32]{1,2,0:T(8,128)S(1)} %get-tuple-element.47) | copy-start | bytes 24580
  456.5 14.8 %copy-start.6 = (f32[1,2,64,64]{2,3,1,0:T(8,128)S(1)}, f32[1,2,64,64]{2,3,1,0:T(8,128)}, u32[]{:S(2)}) copy-start(f32[1,2,64,64]{2,3,1,0:T(8,128)} %get-tuple-element.30) | copy-start | bytes 98308
  456.5 14.8 %copy-start.7 = (f32[1,2,64,64]{2,3,1,0:T(8,128)S(1)}, f32[1,2,64,64]{2,3,1,0:T(8,128)}, u32[]{:S(2)}) copy-start(f32[1,2,64,64]{2,3,1,0:T(8,128)} %get-tuple-element.33) | copy-start | bytes 98308
  465.5 180.6 %all-to-all-start.2 = ((f32[8,512,256]{2,1,0:T(8,128)}), f32[8,512,256]{2,1,0:T(8,128)}, u32[]{:S(2)}, u32[]{:S(2)}) async-start(f32[8,512,256]{2,1,0:T(8,128)} %copy.111), calls=%async_computation.2 | async-start | bytes 8388608 | tf_op jit(solution)/shard_map/all_to_all | solution.py:142
  527.6 19.1 %copy-start.12 = (f32[1,2,64,32]{2,3,0,1:T(8,128)S(1)}, f32[1,2,64,32]{2,3,0,1:T(8,128)}, u32[]{:S(2)}) copy-start(f32[1,2,64,32]{2,3,0,1:T(8,128)} %get-tuple-element.34) | copy-start | bytes 49156
  527.6 19.1 %copy-start.13 = (f32[1,2,64,32]{2,3,0,1:T(8,128)S(1)}, f32[1,2,64,32]{2,3,0,1:T(8,128)}, u32[]{:S(2)}) copy-start(f32[1,2,64,32]{2,3,0,1:T(8,128)} %get-tuple-element.35) | copy-start | bytes 49156
  646.1 190.0 %all-to-all-start = ((f32[2,1,2048,1024]{3,0,1,2:T(2,128)}), f32[2,1,2048,1024]{3,0,1,2:T(2,128)}, u32[]{:S(2)}, u32[]{:S(2)}) async-start(f32[2,1,2048,1024]{3,0,1,2:T(2,128)} %copy.101), calls=%async_computation | async-start | bytes 33554432 | tf_op jit(solution)/shard_map/all_to_all | solution.py:131
  912.4 7.4 copy-start.9
  912.4 7.4 copy-start.11
  919.8 23.2 %copy-start.2 = (f32[1,512,2048]{1,2,0:T(8,128)S(1)}, f32[1,512,2048]{1,2,0:T(8,128)}, u32[]{:S(2)}) copy-start(f32[1,512,2048]{1,2,0:T(8,128)} %copy.113) | copy-start | bytes 12582916
  919.8 23.2 %copy-start.3 = (f32[1,512,8,256]{1,3,2,0:T(8,128)S(1)}, f32[1,512,8,256]{1,3,2,0:T(8,128)}, u32[]{:S(2)}) copy-start(f32[1,512,8,256]{1,3,2,0:T(8,128)} %copy.112) | copy-start | bytes 12582916
  941.0 2.0 copy-start.4
  1044.4 25.7 %copy-start.1 = (f32[8,8]{1,0:T(8,128)S(1)}, f32[8,8]{1,0:T(8,128)}, u32[]{:S(2)}) copy-start(f32[8,8]{1,0:T(8,128)} %param.10) | copy-start | bytes 772
